TPU v7x, 256 devices: a whole 4x4x8 slice. The times are simulated.
256 devices in a mesh: section: 2 (over core), ctx: 128 (over y, z, x).
Axes of the slice: x: 4, y: 4, z: 8, core: 2. Of those that a mesh axis runs over, the one named last changes fastest.
Arguments:
- queries: bfloat16 [2, 8192, 4096], P('section', 'ctx'), may hold values from -80 to 80
- key_rows: bfloat16 [2, 8192, 512], P('section', 'ctx'), may hold values from -8 to 8
- rows_of_value: bfloat16 [2, 8192, 512], P('section', 'ctx'), may hold values from -6 to 6
- query_gain: float32 [4096], replicated, may hold values from 2 to 6
- block_order: int32 [256], replicated, may hold values from 0 to 255, each once
Outputs:
- attended: bfloat16 [2, 8192, 4096], P('section', 'ctx')
Inputs may be any that keep to these rules, and one draw needn't show every extreme that they name: A permutation; stored block j of 32 rows holds the sequence's block block_order[j].
All inputs are finite; a program needn't handle non-finite values.
Results may differ from a plain program's by a relative error of at most 0.0085.
Values may be sent and summed in bfloat16 or wider, within the bound.
A program may use at most 192 MiB of HBM per device.

v0:
```python
import math
import jax
import jax.numpy as jnp
from jax import lax
from jax.sharding import PartitionSpec as P

HEAD_SIZE = 128
QUERY_PER_GROUP = 8


def from_behind(value, axis, steps):
    count = lax.axis_size(axis)
    initial, last = (max(0, -steps), min(count, count - steps))
    return lax.ppermute(value, axis, [(source, source + steps) for source in range(initial, last)])


def key_positions(block_order, first_row_index, row_count, block_rows):
    row_ids = first_row_index + jnp.arange(row_count, dtype=jnp.int32)
    slot_ids = row_ids // block_rows
    slot_table = jnp.arange(block_order.shape[0], dtype=jnp.int32)
    picked = jnp.sum(
        jnp.where(slot_ids[:, None] == slot_table[None, :], block_order[None, :], 0), axis=1
    )
    return picked * block_rows + row_ids % block_rows


def fold_step(carry_state, key_piece, value_piece, key_pos, query_four, query_pos, needed):
    row_count = key_piece.shape[0]
    kv_heads = query_four.shape[1]
    score_scale = 1.0 / math.sqrt(HEAD_SIZE)

    def compute(old_state):
        row_max, row_sum, mixed_sum = old_state
        key_quad = key_piece.reshape(row_count, kv_heads, HEAD_SIZE)
        scores = (
            jnp.einsum("qjgd,kjd->jgqk", query_four, key_quad, preferred_element_type=jnp.float32)
            * score_scale
        )
        scores = jnp.where(key_pos[None, :] <= query_pos[:, None], scores, -jnp.inf)
        new_max = jnp.maximum(row_max, jnp.max(scores, axis=-1))
        rescale = jnp.exp(row_max - new_max)
        weights = jnp.exp(scores - new_max[..., None])
        new_sum = row_sum * rescale + jnp.sum(weights, axis=-1)
        value_four = value_piece.reshape(row_count, kv_heads, HEAD_SIZE)
        product = jnp.einsum(
            "jgqk,kjd->qjgd",
            weights.astype(jnp.bfloat16),
            value_four,
            preferred_element_type=jnp.float32,
        )
        new_mixed = mixed_sum * jnp.transpose(rescale, (2, 0, 1))[..., None] + product
        return (new_max, new_sum, new_mixed)

    return lax.cond(needed, compute, lambda same_state: same_state, carry_state)


def body(queries, key_rows, rows_of_value, query_gain, block_order):
    rows_here = queries.shape[1]
    block_rows = rows_here // 2
    query_pos = key_positions(block_order, lax.axis_index("ctx") * rows_here, rows_here, block_rows)
    section_now = lax.axis_index("section")
    kv_heads = key_rows.shape[2] // HEAD_SIZE
    column_count = queries.shape[2]
    start_state = (
        jnp.full((kv_heads, QUERY_PER_GROUP, rows_here), -1e30, jnp.float32),
        jnp.zeros((kv_heads, QUERY_PER_GROUP, rows_here), jnp.float32),
        jnp.zeros((rows_here, kv_heads, QUERY_PER_GROUP, HEAD_SIZE), jnp.float32),
    )

    def finish(final_state):
        row_max, row_sum, mixed_sum = final_state
        safe_sum = jnp.where(row_sum > 0.0, row_sum, 1.0)
        mixed_out = mixed_sum / jnp.transpose(safe_sum, (2, 0, 1))[..., None]
        return mixed_out.reshape(rows_here, column_count).astype(jnp.bfloat16)

    gathered = (
        lax.all_gather(key_rows, "ctx", axis=1, tiled=True),
        lax.all_gather(rows_of_value, "ctx", axis=1, tiled=True),
    )
    total_rows = gathered[0].shape[1]
    width_of_block = math.gcd(total_rows, 512)

    def attend(rows_of_query, active):
        query_four = rows_of_query.reshape(rows_here, kv_heads, QUERY_PER_GROUP, HEAD_SIZE)

        def loop_body(loop_index, carry_state):
            first_row_index = loop_index * width_of_block
            key_piece = lax.dynamic_slice_in_dim(gathered[0][0], first_row_index, width_of_block, 0)
            value_piece = lax.dynamic_slice_in_dim(
                gathered[1][0], first_row_index, width_of_block, 0
            )
            key_pos = key_positions(block_order, first_row_index, width_of_block, block_rows)
            return fold_step(
                carry_state, key_piece, value_piece, key_pos, query_four, query_pos, active
            )

        return finish(lax.fori_loop(0, total_rows // width_of_block, loop_body, start_state))

    first_out = attend(queries[0], section_now == 0)
    received = from_behind(first_out, "section", 1)
    shifted = (
        queries[0].astype(jnp.float32) + query_gain[None, :] * received.astype(jnp.float32)
    ).astype(jnp.bfloat16)
    second = attend(shifted, section_now == 1)
    result = jnp.where(section_now == 0, first_out, second)
    return result[None]


def solution(mesh):
    placed = (
        P("section", "ctx", None),
        P("section", "ctx", None),
        P("section", "ctx", None),
        P(),
        P(),
    )
    return jax.shard_map(
        body, mesh=mesh, in_specs=placed, out_specs=P("section", "ctx", None), check_vma=False
    )
```

profile of v0, /device:TPU:1, one launch (start us, length us, event | category | flops | bytes accessed | tf_op | source)
XLA Modules:
  0.0 462.5 jit_solution(13137162699228120019)
XLA Ops:
  10.3 125.7 %all-gather.3.cloned.1.call-done = bf16[1,8192,512]{2,1,0:T(8,128)(2,1)} async-done(((bf16[1,64,512]{2,1,0:T(8,128)(2,1)}), bf16[1,8192,512]{2,1,0:T(8,128)(2,1)}) %all-gather.3.cloned.1.call-update) | async-done | bytes 8388624 | tf_op jit(solution)/shard_map/all_gather | solution.py:77
  135.9 12.0 %copy.33 = bf16[1,8192,512]{1,2,0:T(8,128)(2,1)} copy(bf16[1,8192,512]{2,1,0:T(8,128)(2,1)} %all-gather.3.cloned.1.call-done) | data formatting | bytes 16777216 | tf_op jit(solution)/shard_map/while | solution.py:97
  147.9 112.4 %all-gather.5.cloned.1.call-done = bf16[1,8192,512]{2,1,0:T(8,128)(2,1)} async-done(((bf16[1,64,512]{2,1,0:T(8,128)(2,1)}), bf16[1,8192,512]{2,1,0:T(8,128)(2,1)}) %all-gather.5.cloned.1.call-update) | async-done | bytes 8388624 | tf_op jit(solution)/shard_map/all_gather | solution.py:78
  260.3 11.9 %copy.35 = bf16[1,8192,512]{1,2,0:T(8,128)(2,1)} copy(bf16[1,8192,512]{2,1,0:T(8,128)(2,1)} %all-gather.5.cloned.1.call-done) | data formatting | bytes 16777216 | tf_op jit(solution)/shard_map/while | solution.py:97
  272.4 1.7 while.38
  275.1 1.5 collective-permute-start
  276.6 89.6 %collective-permute-done = bf16[64,4096]{1,0:T(8,128)(2,1)S(1)} collective-permute-done((bf16[64,4096]{1,0:T(8,128)(2,1)S(1)}, bf16[64,4096]{1,0:T(8,128)(2,1)S(1)}, u32[]{:S(2)}, u32[]{:S(2)}) %collective-permute-start) | collective-permute-done | bytes 524320 | tf_op jit(solution)/shard_map/ppermute | solution.py:14
  366.7 86.8 %while.39 = (s32[]{:T(128)}, f32[4,8,64]{2,1,0:T(8,128)S(1)}, f32[4,8,64]{2,1,0:T(8,128)S(1)}, f32[64,4,8,128]{3,0,2,1:T(8,128)S(1)}, pred[]{:T(512)}, /*index=5...) while((s32[]{:T(128)}, f32[4,8,64]{2,1,0:T(8,128)S(1)}, ...), condition=%wide.region_14.15_spmd, body=%wide.region_8.14_spmd.sunk | while | flops 549376512 | bytes 19682900 | solution.py:97
  366.8 5.3 %conditional.5 = ((f32[4,8,64]{2,1,0:T(8,128)S(1)}, f32[4,8,64]{2,1,0:T(8,128)S(1)}, f32[64,4,8,128]{3,0,2,1:T(8,128)S(1)})) conditional(s32[]{:T(128)} %convert_element_type.110, (f32[4,8,64]{2,1,0:T(8,128)S(1)}, f32[4,8,64]{2,1,0:T(8,128)S(1)}, f32[64,4,8,128]{3,0,2,1:T(8,128)S(1)}) %tuple.209, (s32[]{:T(128)}, ...), branch_computations={%region_9.9_spmd, %region_10.13_spmd.clone.clone} | conditional | flops 549376512 | bytes 19154254 | solution.py:54
  369.3 1.5 fusion.32
  370.8 1.3 fusion.21
  372.3 5.3 %conditional.5 = ((f32[4,8,64]{2,1,0:T(8,128)S(1)}, f32[4,8,64]{2,1,0:T(8,128)S(1)}, f32[64,4,8,128]{3,0,2,1:T(8,128)S(1)})) conditional(s32[]{:T(128)} %convert_element_type.110, (f32[4,8,64]{2,1,0:T(8,128)S(1)}, f32[4,8,64]{2,1,0:T(8,128)S(1)}, f32[64,4,8,128]{3,0,2,1:T(8,128)S(1)}) %tuple.209, (s32[]{:T(128)}, ...), branch_computations={%region_9.9_spmd, %region_10.13_spmd.clone.clone} | conditional | flops 549376512 | bytes 19154254 | solution.py:54
  374.7 1.5 fusion.32
  376.3 1.3 fusion.21
  377.7 5.3 %conditional.5 = ((f32[4,8,64]{2,1,0:T(8,128)S(1)}, f32[4,8,64]{2,1,0:T(8,128)S(1)}, f32[64,4,8,128]{3,0,2,1:T(8,128)S(1)})) conditional(s32[]{:T(128)} %convert_element_type.110, (f32[4,8,64]{2,1,0:T(8,128)S(1)}, f32[4,8,64]{2,1,0:T(8,128)S(1)}, f32[64,4,8,128]{3,0,2,1:T(8,128)S(1)}) %tuple.209, (s32[]{:T(128)}, ...), branch_computations={%region_9.9_spmd, %region_10.13_spmd.clone.clone} | conditional | flops 549376512 | bytes 19154254 | solution.py:54
  380.2 1.5 fusion.32
  381.7 1.3 fusion.21
  383.1 5.3 %conditional.5 = ((f32[4,8,64]{2,1,0:T(8,128)S(1)}, f32[4,8,64]{2,1,0:T(8,128)S(1)}, f32[64,4,8,128]{3,0,2,1:T(8,128)S(1)})) conditional(s32[]{:T(128)} %convert_element_type.110, (f32[4,8,64]{2,1,0:T(8,128)S(1)}, f32[4,8,64]{2,1,0:T(8,128)S(1)}, f32[64,4,8,128]{3,0,2,1:T(8,128)S(1)}) %tuple.209, (s32[]{:T(128)}, ...), branch_computations={%region_9.9_spmd, %region_10.13_spmd.clone.clone} | conditional | flops 549376512 | bytes 19154254 | solution.py:54
  385.6 1.5 fusion.32
  387.1 1.3 fusion.21
  388.5 5.3 %conditional.5 = ((f32[4,8,64]{2,1,0:T(8,128)S(1)}, f32[4,8,64]{2,1,0:T(8,128)S(1)}, f32[64,4,8,128]{3,0,2,1:T(8,128)S(1)})) conditional(s32[]{:T(128)} %convert_element_type.110, (f32[4,8,64]{2,1,0:T(8,128)S(1)}, f32[4,8,64]{2,1,0:T(8,128)S(1)}, f32[64,4,8,128]{3,0,2,1:T(8,128)S(1)}) %tuple.209, (s32[]{:T(128)}, ...), branch_computations={%region_9.9_spmd, %region_10.13_spmd.clone.clone} | conditional | flops 549376512 | bytes 19154254 | solution.py:54
  391.0 1.5 fusion.32
  392.5 1.3 fusion.21
  394.0 5.3 %conditional.5 = ((f32[4,8,64]{2,1,0:T(8,128)S(1)}, f32[4,8,64]{2,1,0:T(8,128)S(1)}, f32[64,4,8,128]{3,0,2,1:T(8,128)S(1)})) conditional(s32[]{:T(128)} %convert_element_type.110, (f32[4,8,64]{2,1,0:T(8,128)S(1)}, f32[4,8,64]{2,1,0:T(8,128)S(1)}, f32[64,4,8,128]{3,0,2,1:T(8,128)S(1)}) %tuple.209, (s32[]{:T(128)}, ...), branch_computations={%region_9.9_spmd, %region_10.13_spmd.clone.clone} | conditional | flops 549376512 | bytes 19154254 | solution.py:54
  396.4 1.5 fusion.32
  397.9 1.3 fusion.21
  399.4 5.3 %conditional.5 = ((f32[4,8,64]{2,1,0:T(8,128)S(1)}, f32[4,8,64]{2,1,0:T(8,128)S(1)}, f32[64,4,8,128]{3,0,2,1:T(8,128)S(1)})) conditional(s32[]{:T(128)} %convert_element_type.110, (f32[4,8,64]{2,1,0:T(8,128)S(1)}, f32[4,8,64]{2,1,0:T(8,128)S(1)}, f32[64,4,8,128]{3,0,2,1:T(8,128)S(1)}) %tuple.209, (s32[]{:T(128)}, ...), branch_computations={%region_9.9_spmd, %region_10.13_spmd.clone.clone} | conditional | flops 549376512 | bytes 19154254 | solution.py:54
  401.8 1.5 fusion.32
  404.8 5.3 %conditional.5 = ((f32[4,8,64]{2,1,0:T(8,128)S(1)}, f32[4,8,64]{2,1,0:T(8,128)S(1)}, f32[64,4,8,128]{3,0,2,1:T(8,128)S(1)})) conditional(s32[]{:T(128)} %convert_element_type.110, (f32[4,8,64]{2,1,0:T(8,128)S(1)}, f32[4,8,64]{2,1,0:T(8,128)S(1)}, f32[64,4,8,128]{3,0,2,1:T(8,128)S(1)}) %tuple.209, (s32[]{:T(128)}, ...), branch_computations={%region_9.9_spmd, %region_10.13_spmd.clone.clone} | conditional | flops 549376512 | bytes 19154254 | solution.py:54
  407.3 1.5 fusion.32
  410.2 5.3 %conditional.5 = ((f32[4,8,64]{2,1,0:T(8,128)S(1)}, f32[4,8,64]{2,1,0:T(8,128)S(1)}, f32[64,4,8,128]{3,0,2,1:T(8,128)S(1)})) conditional(s32[]{:T(128)} %convert_element_type.110, (f32[4,8,64]{2,1,0:T(8,128)S(1)}, f32[4,8,64]{2,1,0:T(8,128)S(1)}, f32[64,4,8,128]{3,0,2,1:T(8,128)S(1)}) %tuple.209, (s32[]{:T(128)}, ...), branch_computations={%region_9.9_spmd, %region_10.13_spmd.clone.clone} | conditional | flops 549376512 | bytes 19154254 | solution.py:54
  412.7 1.5 fusion.32
  415.6 5.3 %conditional.5 = ((f32[4,8,64]{2,1,0:T(8,128)S(1)}, f32[4,8,64]{2,1,0:T(8,128)S(1)}, f32[64,4,8,128]{3,0,2,1:T(8,128)S(1)})) conditional(s32[]{:T(128)} %convert_element_type.110, (f32[4,8,64]{2,1,0:T(8,128)S(1)}, f32[4,8,64]{2,1,0:T(8,128)S(1)}, f32[64,4,8,128]{3,0,2,1:T(8,128)S(1)}) %tuple.209, (s32[]{:T(128)}, ...), branch_computations={%region_9.9_spmd, %region_10.13_spmd.clone.clone} | conditional | flops 549376512 | bytes 19154254 | solution.py:54
  418.1 1.5 fusion.32
  421.1 5.3 %conditional.5 = ((f32[4,8,64]{2,1,0:T(8,128)S(1)}, f32[4,8,64]{2,1,0:T(8,128)S(1)}, f32[64,4,8,128]{3,0,2,1:T(8,128)S(1)})) conditional(s32[]{:T(128)} %convert_element_type.110, (f32[4,8,64]{2,1,0:T(8,128)S(1)}, f32[4,8,64]{2,1,0:T(8,128)S(1)}, f32[64,4,8,128]{3,0,2,1:T(8,128)S(1)}) %tuple.209, (s32[]{:T(128)}, ...), branch_computations={%region_9.9_spmd, %region_10.13_spmd.clone.clone} | conditional | flops 549376512 | bytes 19154254 | solution.py:54
  423.5 1.5 fusion.32
  426.5 5.3 %conditional.5 = ((f32[4,8,64]{2,1,0:T(8,128)S(1)}, f32[4,8,64]{2,1,0:T(8,128)S(1)}, f32[64,4,8,128]{3,0,2,1:T(8,128)S(1)})) conditional(s32[]{:T(128)} %convert_element_type.110, (f32[4,8,64]{2,1,0:T(8,128)S(1)}, f32[4,8,64]{2,1,0:T(8,128)S(1)}, f32[64,4,8,128]{3,0,2,1:T(8,128)S(1)}) %tuple.209, (s32[]{:T(128)}, ...), branch_computations={%region_9.9_spmd, %region_10.13_spmd.clone.clone} | conditional | flops 549376512 | bytes 19154254 | solution.py:54
  429.0 1.5 fusion.32
  431.9 5.3 %conditional.5 = ((f32[4,8,64]{2,1,0:T(8,128)S(1)}, f32[4,8,64]{2,1,0:T(8,128)S(1)}, f32[64,4,8,128]{3,0,2,1:T(8,128)S(1)})) conditional(s32[]{:T(128)} %convert_element_type.110, (f32[4,8,64]{2,1,0:T(8,128)S(1)}, f32[4,8,64]{2,1,0:T(8,128)S(1)}, f32[64,4,8,128]{3,0,2,1:T(8,128)S(1)}) %tuple.209, (s32[]{:T(128)}, ...), branch_computations={%region_9.9_spmd, %region_10.13_spmd.clone.clone} | conditional | flops 549376512 | bytes 19154254 | solution.py:54
  434.4 1.5 fusion.32
  435.9 1.3 fusion.21
  437.3 5.3 %conditional.5 = ((f32[4,8,64]{2,1,0:T(8,128)S(1)}, f32[4,8,64]{2,1,0:T(8,128)S(1)}, f32[64,4,8,128]{3,0,2,1:T(8,128)S(1)})) conditional(s32[]{:T(128)} %convert_element_type.110, (f32[4,8,64]{2,1,0:T(8,128)S(1)}, f32[4,8,64]{2,1,0:T(8,128)S(1)}, f32[64,4,8,128]{3,0,2,1:T(8,128)S(1)}) %tuple.209, (s32[]{:T(128)}, ...), branch_computations={%region_9.9_spmd, %region_10.13_spmd.clone.clone} | conditional | flops 549376512 | bytes 19154254 | solution.py:54
  439.8 1.5 fusion.32
  441.3 1.3 fusion.21
  442.8 5.3 %conditional.5 = ((f32[4,8,64]{2,1,0:T(8,128)S(1)}, f32[4,8,64]{2,1,0:T(8,128)S(1)}, f32[64,4,8,128]{3,0,2,1:T(8,128)S(1)})) conditional(s32[]{:T(128)} %convert_element_type.110, (f32[4,8,64]{2,1,0:T(8,128)S(1)}, f32[4,8,64]{2,1,0:T(8,128)S(1)}, f32[64,4,8,128]{3,0,2,1:T(8,128)S(1)}) %tuple.209, (s32[]{:T(128)}, ...), branch_computations={%region_9.9_spmd, %region_10.13_spmd.clone.clone} | conditional | flops 549376512 | bytes 19154254 | solution.py:54
  445.2 1.5 fusion.32
  448.2 5.3 %conditional.5 = ((f32[4,8,64]{2,1,0:T(8,128)S(1)}, f32[4,8,64]{2,1,0:T(8,128)S(1)}, f32[64,4,8,128]{3,0,2,1:T(8,128)S(1)})) conditional(s32[]{:T(128)} %convert_element_type.110, (f32[4,8,64]{2,1,0:T(8,128)S(1)}, f32[4,8,64]{2,1,0:T(8,128)S(1)}, f32[64,4,8,128]{3,0,2,1:T(8,128)S(1)}) %tuple.209, (s32[]{:T(128)}, ...), branch_computations={%region_9.9_spmd, %region_10.13_spmd.clone.clone} | conditional | flops 549376512 | bytes 19154254 | solution.py:54
  450.7 1.5 fusion.32
  (296 shorter events, 58.4 us)
Async XLA Ops:
  6.5 129.4 %all-gather.3.cloned.1.call-start = ((), (), s32[]{:S(2)}) async-start(), calls=%async_computation | async-start | bytes 8454144 | tf_op jit(solution)/shard_map/all_gather | solution.py:77
  7.3 253.0 %all-gather.5.cloned.1.call-start = ((), (), s32[]{:S(2)}) async-start(), calls=%async_computation.1 | async-start | bytes 8454144 | tf_op jit(solution)/shard_map/all_gather | solution.py:78
  147.9 124.5 %copy-start.1 = (s32[256]{0:T(256)S(1)}, s32[256]{0:T(256)}, u32[]{:S(2)}) copy-start(s32[256]{0:T(256)} %param.17) | copy-start | bytes 3076
  272.4 93.7 %copy-start = (bf16[1,64,4096]{2,1,0:T(8,128)(2,1)S(1)}, bf16[1,64,4096]{2,1,0:T(8,128)(2,1)}, u32[]{:S(2)}) copy-start(bf16[1,64,4096]{2,1,0:T(8,128)(2,1)} %param.13) | copy-start | bytes 1572868
  272.4 93.7 %copy-start.2 = (f32[4096]{0:T(1024)S(1)}, f32[4096]{0:T(1024)}, u32[]{:S(2)}) copy-start(f32[4096]{0:T(1024)} %param.16) | copy-start | bytes 49156
  275.1 91.0 %collective-permute-start = (bf16[64,4096]{1,0:T(8,128)(2,1)S(1)}, bf16[64,4096]{1,0:T(8,128)(2,1)S(1)}, u32[]{:S(2)}, u32[]{:S(2)}) collective-permute-start(bf16[64,4096]{1,0:T(8,128)(2,1)S(1)} %bitcast.108), channel_id=1, source_target_pairs={{0,128},{1,129},{2,130},{3,131},{4,132},{5,133},{6,134},{7,135},{8... | collective-permute-start | bytes 1572872 | tf_op jit(solution)/shard_map/ppermute | solution.py:14
Sparse Core Ops, SparseCore 0:
  11.0 124.9 all-gather.2
  139.5 120.6 all-gather.4
where the time goes:
time: 464 us; the launch traced here: 462 us
  waiting for transfers between devices  329 us (71%)
  local copies, waits for them, and re-layouts  49.6 us (11%)
  matrix products  36.7 us (8%)
  other arithmetic  29 us (6%)
  between operations  13.6 us (3%)
    all_gather x1, waiting for transfers between devices, body(): lax.all_gather(key_rows, 'ctx', axis=1, tiled=True)  126 us
    all_gather x1, waiting for transfers between devices, body(): lax.all_gather(rows_of_value, 'ctx', axis=1, tiled=True)  112 us
    ppermute x1, waiting for transfers between devices, from_behind(): lax.ppermute(value, axis, [(source, source + steps) for source in range(i...  89.6 us
    while x4, local copies, waits for them, and re-layouts, attend(): lax.fori_loop(0, total_rows // width_of_block, loop_body, start_state)  24.3 us
    dot_general x16, matrix products, compute(): jnp.einsum('jgqk,kjd->qjgd', weights.astype(jnp.bfloat16), value_four, pr...  24.2 us
    reduce_sum x16, other arithmetic, compute(): new_sum = row_sum * rescale + jnp.sum(weights, axis=-1)  20.8 us
    dynamic_slice x16, local copies, waits for them, and re-layouts, loop_body(): lax.dynamic_slice_in_dim(gathered[0][0], first_row_index, width_of_block, 0)  20.4 us
    dot_general x16, matrix products, compute(): jnp.einsum('qjgd,kjd->jgqk', query_four, key_quad, preferred_element_type...  12.4 us
  transfers between devices with their start and end apart: 3, of which 3 were waited for; matrix products, arithmetic and copies ran while one was open for 3% of the time, Pallas kernels for 0%

commit v1 on v0

--- a/solution.py
+++ b/solution.py
@@ -6,6 +6,9 @@
 
 HEAD_SIZE = 128
 QUERY_PER_GROUP = 8
+take_circles = lambda axis_name, inp: jnp.concatenate(
+    lax.all_to_all(jnp.stack([inp] * lax.axis_size(axis_name)), axis_name, 0, 0), 1
+)
 
 
 def from_behind(value, axis, steps):
@@ -75,7 +78,7 @@
 
     gathered = (
         lax.all_gather(key_rows, "ctx", axis=1, tiled=True),
-        lax.all_gather(rows_of_value, "ctx", axis=1, tiled=True),
+        take_circles("ctx", rows_of_value),
     )
     total_rows = gathered[0].shape[1]
     width_of_block = math.gcd(total_rows, 512)

time: 464 us -> 622 us (1.34)
  matrix products: 36.7 us -> 119 us
  waiting for transfers between devices: 329 us -> 376 us
  starting transfers between devices: 1.51 us -> 18.5 us
  local copies, waits for them, and re-layouts: 49.6 us -> 60.4 us
    all_gather x1 -> x0, waiting for transfers between devices: 112 us -> none  [body(): lax.all_gather(rows_of_value, 'ctx', axis=1, tiled=True)]
    ppermute x1, waiting for transfers between devices: 89.6 us -> 171 us  [from_behind(): lax.ppermute(value, axis, [(source, source + steps) for source in range(i...]
    all_gather x1, waiting for transfers between devices: 126 us -> 201 us  [body(): lax.all_gather(key_rows, 'ctx', axis=1, tiled=True)]
    dot_general x16, matrix products: 24.2 us -> 77.3 us  [compute(): jnp.einsum('jgqk,kjd->qjgd', weights.astype(jnp.bfloat16), value_four, pr...]
    dot_general x16, matrix products: 12.4 us -> 42.1 us  [compute(): jnp.einsum('qjgd,kjd->jgqk', query_four, key_quad, preferred_element_type...]
    dynamic_slice x0 -> x32, local copies, waits for them, and re-layouts: none -> 20.7 us  [loop_body(): lax.dynamic_slice_in_dim(gathered[1][0], first_row_index, width_of_block, 0)]
    all_to_all x0 -> x1, starting transfers between devices: none -> 17 us  [lax.all_to_all(jnp.stack([inp] * lax.axis_size(axis_name)), axis_name, 0, 0)]
    while x4 -> x3, local copies, waits for them, and re-layouts: 24.3 us -> 12.3 us  [attend(): lax.fori_loop(0, total_rows // width_of_block, loop_body, start_state)]
where the time goes in v1:
time: 622 us; the launch traced here: 620 us
  waiting for transfers between devices  376 us (60%)
  matrix products  119 us (19%)
  local copies, waits for them, and re-layouts  60.4 us (10%)
  other arithmetic  29.3 us (5%)
  starting transfers between devices  18.5 us (3%)
  between operations  13.6 us (2%)
    all_gather x1, waiting for transfers between devices, body(): lax.all_gather(key_rows, 'ctx', axis=1, tiled=True)  201 us
    ppermute x1, waiting for transfers between devices, from_behind(): lax.ppermute(value, axis, [(source, source + steps) for source in range(i...  171 us
    dot_general x16, matrix products, compute(): jnp.einsum('jgqk,kjd->qjgd', weights.astype(jnp.bfloat16), value_four, pr...  77.3 us
    dot_general x16, matrix products, compute(): jnp.einsum('qjgd,kjd->jgqk', query_four, key_quad, preferred_element_type...  42.1 us
    reduce_sum x16, other arithmetic, compute(): new_sum = row_sum * rescale + jnp.sum(weights, axis=-1)  20.8 us
    dynamic_slice x32, local copies, waits for them, and re-layouts, loop_body(): lax.dynamic_slice_in_dim(gathered[1][0], first_row_index, width_of_block, 0)  20.7 us
    dynamic_slice x16, local copies, waits for them, and re-layouts, loop_body(): lax.dynamic_slice_in_dim(gathered[0][0], first_row_index, width_of_block, 0)  17.3 us
    all_to_all x1, starting transfers between devices, lax.all_to_all(jnp.stack([inp] * lax.axis_size(axis_name)), axis_name, 0, 0)  17 us
  transfers between devices with their start and end apart: 3, of which 3 were waited for; matrix products, arithmetic and copies ran while one was open for 3% of the time, Pallas kernels for 0%

profile of v1, /device:TPU:1, one launch (start us, length us, event | category | flops | bytes accessed | tf_op | source)
XLA Modules:
  0.0 620.4 jit_solution(13365061019495883905)
XLA Ops:
  7.3 5.1 stack.2
  12.4 17.0 %all-to-all-start = ((bf16[128,1,64,512]{3,2,1,0:T(8,128)(2,1)}), bf16[128,1,64,512]{3,2,1,0:T(8,128)(2,1)}, u32[]{:S(2)}, u32[]{:S(2)}) async-start(bf16[128,1,64,512]{3,2,1,0:T(8,128)(2,1)} %stack.2), calls=%async_computation | async-start | bytes 16777216 | tf_op jit(solution)/shard_map/all_to_all | solution.py:10
  29.9 201.2 %all-gather.2.cloned.1.call-done = bf16[1,8192,512]{2,1,0:T(8,128)(2,1)} async-done(((bf16[1,64,512]{2,1,0:T(8,128)(2,1)}), bf16[1,8192,512]{2,1,0:T(8,128)(2,1)}) %all-gather.2.cloned.1.call-update) | async-done | bytes 8388624 | tf_op jit(solution)/shard_map/all_gather | solution.py:80
  231.1 11.9 %copy.48 = bf16[1,8192,512]{1,2,0:T(8,128)(2,1)} copy(bf16[1,8192,512]{2,1,0:T(8,128)(2,1)} %all-gather.2.cloned.1.call-done) | data formatting | bytes 16777216 | tf_op jit(solution)/shard_map/while | solution.py:100
  243.0 2.7 all-to-all-done
  250.1 171.5 %collective-permute-done = bf16[64,4096]{1,0:T(8,128)(2,1)S(1)} collective-permute-done((bf16[64,4096]{1,0:T(8,128)(2,1)S(1)}, bf16[64,4096]{1,0:T(8,128)(2,1)S(1)}, u32[]{:S(2)}, u32[]{:S(2)}) %collective-permute-start) | collective-permute-done | bytes 524320 | tf_op jit(solution)/shard_map/ppermute | solution.py:17
  423.1 187.3 %while.39 = (s32[]{:T(128)}, f32[4,8,64]{2,1,0:T(8,128)S(1)}, f32[4,8,64]{2,1,0:T(8,128)S(1)}, f32[64,4,8,128]{3,0,2,1:T(8,128)}, pred[]{:T(512)}, /*index=5*/s3...) while((s32[]{:T(128)}, f32[4,8,64]{2,1,0:T(8,128)S(1)}, ...), condition=%wide.region_14.15_spmd, body=%wide.region_8.14_spmd.sunk | while | flops 549376512 | bytes 37508724 | solution.py:100
  423.2 11.6 %conditional.5 = ((f32[4,8,64]{2,1,0:T(8,128)S(1)}, f32[4,8,64]{2,1,0:T(8,128)S(1)}, f32[64,4,8,128]{3,0,2,1:T(8,128)})) conditional(s32[]{:T(128)} %convert_element_type.110, (f32[4,8,64]{2,1,0:T(8,128)S(1)}, f32[4,8,64]{2,1,0:T(8,128)S(1)}, f32[64,4,8,128]{3,0,2,1:T(8,128)}) %tuple.209, (s32[]{:T(128)}, s32[512,1]{0,1:T(1,128)S(1)}, ...), branch_computations={%region_9.9_spmd, %region_10.13_spmd.clone.clone} | conditional | flops 549376512 | bytes 36980080 | solution.py:57
  428.7 4.8 fusion.32
  434.9 11.6 %conditional.5 = ((f32[4,8,64]{2,1,0:T(8,128)S(1)}, f32[4,8,64]{2,1,0:T(8,128)S(1)}, f32[64,4,8,128]{3,0,2,1:T(8,128)})) conditional(s32[]{:T(128)} %convert_element_type.110, (f32[4,8,64]{2,1,0:T(8,128)S(1)}, f32[4,8,64]{2,1,0:T(8,128)S(1)}, f32[64,4,8,128]{3,0,2,1:T(8,128)}) %tuple.209, (s32[]{:T(128)}, s32[512,1]{0,1:T(1,128)S(1)}, ...), branch_computations={%region_9.9_spmd, %region_10.13_spmd.clone.clone} | conditional | flops 549376512 | bytes 36980080 | solution.py:57
  436.4 2.6 fusion.22
  440.4 4.8 fusion.32
  446.6 11.6 %conditional.5 = ((f32[4,8,64]{2,1,0:T(8,128)S(1)}, f32[4,8,64]{2,1,0:T(8,128)S(1)}, f32[64,4,8,128]{3,0,2,1:T(8,128)})) conditional(s32[]{:T(128)} %convert_element_type.110, (f32[4,8,64]{2,1,0:T(8,128)S(1)}, f32[4,8,64]{2,1,0:T(8,128)S(1)}, f32[64,4,8,128]{3,0,2,1:T(8,128)}) %tuple.209, (s32[]{:T(128)}, s32[512,1]{0,1:T(1,128)S(1)}, ...), branch_computations={%region_9.9_spmd, %region_10.13_spmd.clone.clone} | conditional | flops 549376512 | bytes 36980080 | solution.py:57
  448.1 2.6 fusion.22
  452.1 4.8 fusion.32
  458.3 11.6 %conditional.5 = ((f32[4,8,64]{2,1,0:T(8,128)S(1)}, f32[4,8,64]{2,1,0:T(8,128)S(1)}, f32[64,4,8,128]{3,0,2,1:T(8,128)})) conditional(s32[]{:T(128)} %convert_element_type.110, (f32[4,8,64]{2,1,0:T(8,128)S(1)}, f32[4,8,64]{2,1,0:T(8,128)S(1)}, f32[64,4,8,128]{3,0,2,1:T(8,128)}) %tuple.209, (s32[]{:T(128)}, s32[512,1]{0,1:T(1,128)S(1)}, ...), branch_computations={%region_9.9_spmd, %region_10.13_spmd.clone.clone} | conditional | flops 549376512 | bytes 36980080 | solution.py:57
  463.8 4.8 fusion.32
  470.0 11.6 %conditional.5 = ((f32[4,8,64]{2,1,0:T(8,128)S(1)}, f32[4,8,64]{2,1,0:T(8,128)S(1)}, f32[64,4,8,128]{3,0,2,1:T(8,128)})) conditional(s32[]{:T(128)} %convert_element_type.110, (f32[4,8,64]{2,1,0:T(8,128)S(1)}, f32[4,8,64]{2,1,0:T(8,128)S(1)}, f32[64,4,8,128]{3,0,2,1:T(8,128)}) %tuple.209, (s32[]{:T(128)}, s32[512,1]{0,1:T(1,128)S(1)}, ...), branch_computations={%region_9.9_spmd, %region_10.13_spmd.clone.clone} | conditional | flops 549376512 | bytes 36980080 | solution.py:57
  471.5 2.6 fusion.22
  475.5 4.8 fusion.32
  481.7 11.6 %conditional.5 = ((f32[4,8,64]{2,1,0:T(8,128)S(1)}, f32[4,8,64]{2,1,0:T(8,128)S(1)}, f32[64,4,8,128]{3,0,2,1:T(8,128)})) conditional(s32[]{:T(128)} %convert_element_type.110, (f32[4,8,64]{2,1,0:T(8,128)S(1)}, f32[4,8,64]{2,1,0:T(8,128)S(1)}, f32[64,4,8,128]{3,0,2,1:T(8,128)}) %tuple.209, (s32[]{:T(128)}, s32[512,1]{0,1:T(1,128)S(1)}, ...), branch_computations={%region_9.9_spmd, %region_10.13_spmd.clone.clone} | conditional | flops 549376512 | bytes 36980080 | solution.py:57
  483.2 2.6 fusion.22
  487.2 4.8 fusion.32
  493.4 11.6 %conditional.5 = ((f32[4,8,64]{2,1,0:T(8,128)S(1)}, f32[4,8,64]{2,1,0:T(8,128)S(1)}, f32[64,4,8,128]{3,0,2,1:T(8,128)})) conditional(s32[]{:T(128)} %convert_element_type.110, (f32[4,8,64]{2,1,0:T(8,128)S(1)}, f32[4,8,64]{2,1,0:T(8,128)S(1)}, f32[64,4,8,128]{3,0,2,1:T(8,128)}) %tuple.209, (s32[]{:T(128)}, s32[512,1]{0,1:T(1,128)S(1)}, ...), branch_computations={%region_9.9_spmd, %region_10.13_spmd.clone.clone} | conditional | flops 549376512 | bytes 36980080 | solution.py:57
  494.9 2.6 fusion.22
  498.9 4.8 fusion.32
  505.2 11.6 %conditional.5 = ((f32[4,8,64]{2,1,0:T(8,128)S(1)}, f32[4,8,64]{2,1,0:T(8,128)S(1)}, f32[64,4,8,128]{3,0,2,1:T(8,128)})) conditional(s32[]{:T(128)} %convert_element_type.110, (f32[4,8,64]{2,1,0:T(8,128)S(1)}, f32[4,8,64]{2,1,0:T(8,128)S(1)}, f32[64,4,8,128]{3,0,2,1:T(8,128)}) %tuple.209, (s32[]{:T(128)}, s32[512,1]{0,1:T(1,128)S(1)}, ...), branch_computations={%region_9.9_spmd, %region_10.13_spmd.clone.clone} | conditional | flops 549376512 | bytes 36980080 | solution.py:57
  510.6 4.8 fusion.32
  516.9 11.6 %conditional.5 = ((f32[4,8,64]{2,1,0:T(8,128)S(1)}, f32[4,8,64]{2,1,0:T(8,128)S(1)}, f32[64,4,8,128]{3,0,2,1:T(8,128)})) conditional(s32[]{:T(128)} %convert_element_type.110, (f32[4,8,64]{2,1,0:T(8,128)S(1)}, f32[4,8,64]{2,1,0:T(8,128)S(1)}, f32[64,4,8,128]{3,0,2,1:T(8,128)}) %tuple.209, (s32[]{:T(128)}, s32[512,1]{0,1:T(1,128)S(1)}, ...), branch_computations={%region_9.9_spmd, %region_10.13_spmd.clone.clone} | conditional | flops 549376512 | bytes 36980080 | solution.py:57
  518.3 2.6 fusion.22
  522.3 4.8 fusion.32
  528.6 11.6 %conditional.5 = ((f32[4,8,64]{2,1,0:T(8,128)S(1)}, f32[4,8,64]{2,1,0:T(8,128)S(1)}, f32[64,4,8,128]{3,0,2,1:T(8,128)})) conditional(s32[]{:T(128)} %convert_element_type.110, (f32[4,8,64]{2,1,0:T(8,128)S(1)}, f32[4,8,64]{2,1,0:T(8,128)S(1)}, f32[64,4,8,128]{3,0,2,1:T(8,128)}) %tuple.209, (s32[]{:T(128)}, s32[512,1]{0,1:T(1,128)S(1)}, ...), branch_computations={%region_9.9_spmd, %region_10.13_spmd.clone.clone} | conditional | flops 549376512 | bytes 36980080 | solution.py:57
  534.0 4.8 fusion.32
  540.3 11.6 %conditional.5 = ((f32[4,8,64]{2,1,0:T(8,128)S(1)}, f32[4,8,64]{2,1,0:T(8,128)S(1)}, f32[64,4,8,128]{3,0,2,1:T(8,128)})) conditional(s32[]{:T(128)} %convert_element_type.110, (f32[4,8,64]{2,1,0:T(8,128)S(1)}, f32[4,8,64]{2,1,0:T(8,128)S(1)}, f32[64,4,8,128]{3,0,2,1:T(8,128)}) %tuple.209, (s32[]{:T(128)}, s32[512,1]{0,1:T(1,128)S(1)}, ...), branch_computations={%region_9.9_spmd, %region_10.13_spmd.clone.clone} | conditional | flops 549376512 | bytes 36980080 | solution.py:57
  541.7 2.6 fusion.22
  545.7 4.8 fusion.32
  552.0 11.6 %conditional.5 = ((f32[4,8,64]{2,1,0:T(8,128)S(1)}, f32[4,8,64]{2,1,0:T(8,128)S(1)}, f32[64,4,8,128]{3,0,2,1:T(8,128)})) conditional(s32[]{:T(128)} %convert_element_type.110, (f32[4,8,64]{2,1,0:T(8,128)S(1)}, f32[4,8,64]{2,1,0:T(8,128)S(1)}, f32[64,4,8,128]{3,0,2,1:T(8,128)}) %tuple.209, (s32[]{:T(128)}, s32[512,1]{0,1:T(1,128)S(1)}, ...), branch_computations={%region_9.9_spmd, %region_10.13_spmd.clone.clone} | conditional | flops 549376512 | bytes 36980080 | solution.py:57
  557.4 4.8 fusion.32
  563.7 11.6 %conditional.5 = ((f32[4,8,64]{2,1,0:T(8,128)S(1)}, f32[4,8,64]{2,1,0:T(8,128)S(1)}, f32[64,4,8,128]{3,0,2,1:T(8,128)})) conditional(s32[]{:T(128)} %convert_element_type.110, (f32[4,8,64]{2,1,0:T(8,128)S(1)}, f32[4,8,64]{2,1,0:T(8,128)S(1)}, f32[64,4,8,128]{3,0,2,1:T(8,128)}) %tuple.209, (s32[]{:T(128)}, s32[512,1]{0,1:T(1,128)S(1)}, ...), branch_computations={%region_9.9_spmd, %region_10.13_spmd.clone.clone} | conditional | flops 549376512 | bytes 36980080 | solution.py:57
  565.2 2.6 fusion.22
  569.1 4.8 fusion.32
  575.4 11.6 %conditional.5 = ((f32[4,8,64]{2,1,0:T(8,128)S(1)}, f32[4,8,64]{2,1,0:T(8,128)S(1)}, f32[64,4,8,128]{3,0,2,1:T(8,128)})) conditional(s32[]{:T(128)} %convert_element_type.110, (f32[4,8,64]{2,1,0:T(8,128)S(1)}, f32[4,8,64]{2,1,0:T(8,128)S(1)}, f32[64,4,8,128]{3,0,2,1:T(8,128)}) %tuple.209, (s32[]{:T(128)}, s32[512,1]{0,1:T(1,128)S(1)}, ...), branch_computations={%region_9.9_spmd, %region_10.13_spmd.clone.clone} | conditional | flops 549376512 | bytes 36980080 | solution.py:57
  580.8 4.8 fusion.32
  587.1 11.6 %conditional.5 = ((f32[4,8,64]{2,1,0:T(8,128)S(1)}, f32[4,8,64]{2,1,0:T(8,128)S(1)}, f32[64,4,8,128]{3,0,2,1:T(8,128)})) conditional(s32[]{:T(128)} %convert_element_type.110, (f32[4,8,64]{2,1,0:T(8,128)S(1)}, f32[4,8,64]{2,1,0:T(8,128)S(1)}, f32[64,4,8,128]{3,0,2,1:T(8,128)}) %tuple.209, (s32[]{:T(128)}, s32[512,1]{0,1:T(1,128)S(1)}, ...), branch_computations={%region_9.9_spmd, %region_10.13_spmd.clone.clone} | conditional | flops 549376512 | bytes 36980080 | solution.py:57
  588.6 2.6 fusion.22
  592.5 4.8 fusion.32
  598.8 11.6 %conditional.5 = ((f32[4,8,64]{2,1,0:T(8,128)S(1)}, f32[4,8,64]{2,1,0:T(8,128)S(1)}, f32[64,4,8,128]{3,0,2,1:T(8,128)})) conditional(s32[]{:T(128)} %convert_element_type.110, (f32[4,8,64]{2,1,0:T(8,128)S(1)}, f32[4,8,64]{2,1,0:T(8,128)S(1)}, f32[64,4,8,128]{3,0,2,1:T(8,128)}) %tuple.209, (s32[]{:T(128)}, s32[512,1]{0,1:T(1,128)S(1)}, ...), branch_computations={%region_9.9_spmd, %region_10.13_spmd.clone.clone} | conditional | flops 549376512 | bytes 36980080 | solution.py:57
  604.2 4.8 fusion.32
  (359 shorter events, 95.2 us)
Async XLA Ops:
  6.5 224.6 %all-gather.2.cloned.1.call-start = ((), (), s32[]{:S(2)}) async-start(), calls=%async_computation.1 | async-start | bytes 8454144 | tf_op jit(solution)/shard_map/all_gather | solution.py:80
  12.4 17.0 %copy-start.2 = (bf16[1,64,4096]{2,1,0:T(8,128)(2,1)S(1)}, bf16[1,64,4096]{2,1,0:T(8,128)(2,1)}, u32[]{:S(2)}) copy-start(bf16[1,64,4096]{2,1,0:T(8,128)(2,1)} %param.13) | copy-start | bytes 1572868
  12.4 17.4 %copy-start.3 = (s32[256]{0:T(256)S(1)}, s32[256]{0:T(256)}, u32[]{:S(2)}) copy-start(s32[256]{0:T(256)} %param.17) | copy-start | bytes 3076
  12.4 233.4 %all-to-all-start = ((bf16[128,1,64,512]{3,2,1,0:T(8,128)(2,1)}), bf16[128,1,64,512]{3,2,1,0:T(8,128)(2,1)}, u32[]{:S(2)}, u32[]{:S(2)}) async-start(bf16[128,1,64,512]{3,2,1,0:T(8,128)(2,1)} %stack.2), calls=%async_computation | async-start | bytes 16777216 | tf_op jit(solution)/shard_map/all_to_all | solution.py:10
  245.9 175.7 %copy-start.4 = (f32[4096]{0:T(1024)S(1)}, f32[4096]{0:T(1024)}, u32[]{:S(2)}) copy-start(f32[4096]{0:T(1024)} %param.16) | copy-start | bytes 49156
  248.6 173.0 %collective-permute-start = (bf16[64,4096]{1,0:T(8,128)(2,1)S(1)}, bf16[64,4096]{1,0:T(8,128)(2,1)S(1)}, u32[]{:S(2)}, u32[]{:S(2)}) collective-permute-start(bf16[64,4096]{1,0:T(8,128)(2,1)S(1)} %bitcast.115), channel_id=1, source_target_pairs={{0,128},{1,129},{2,130},{3,131},{4,132},{5,133},{6,134},{7,135},{8... | collective-permute-start | bytes 1572872 | tf_op jit(solution)/shard_map/ppermute | solution.py:17
  428.6 4.8 copy-start.1
  440.3 4.8 copy-start.1
  452.1 4.8 copy-start.1
  463.8 4.8 copy-start.1
  475.5 4.8 copy-start.1
  487.2 4.8 copy-start.1
  498.9 4.8 copy-start.1
  510.6 4.8 copy-start.1
  522.3 4.8 copy-start.1
  534.0 4.8 copy-start.1
  545.7 4.8 copy-start.1
  557.4 4.8 copy-start.1
  569.1 4.8 copy-start.1
  580.8 4.8 copy-start.1
  592.5 4.8 copy-start.1
  604.2 4.8 copy-start.1
Sparse Core Ops, SparseCore 0:
  11.0 220.0 all-gather.1
